TPU v7x, 32 devices: a whole 2x2x4 slice. The times are simulated.
32 devices in a mesh: groups: 2 (over x), band: 8 (over z, y), sub: 2 (over core).
Axes of the slice: x: 2, y: 2, z: 4, core: 2. Of those that a mesh axis runs over, the one named last changes fastest.
Arguments:
- sky_maps: bfloat16 [32, 2, 32, 16384], P(('groups', 'band', 'sub')), parts along dimension 0, may hold values from -6 to 6
- sky_mask: float32 [32, 16384], P(('groups', 'band', 'sub')), parts along dimension 0, may hold values from 0.005 to 1, as said below
- pixel_counts: int32 [32], P(('groups', 'band', 'sub')), parts along dimension 0, may hold values from 8192 to 16384, as said below
- phi_offsets: int32 [32], P(('groups', 'band', 'sub')), parts along dimension 0, may hold values from 0 to 1
- low_orders: int32 [32], P('groups'), parts along dimension 0, may hold values from 1 to 4095, as said below
- legendre: bfloat16 [32, 8192, 32], P(('groups', 'band', 'sub')), parts along dimension 0, may hold values from -1 to 1
Outputs:
- alm_packed: float32 [32, 8192, 128], P(('groups', 'band', 'sub')), parts along dimension 0
- spectra: float32 [16384, 2, 1024], P(('groups', 'band', 'sub')), parts along dimension 0
There are 2 independent parts, one for each index of `groups`. A program takes and returns all parts, laid end to end along the dimension named above; each array names one. Nothing has to cross between parts.
Inputs may be any that keep to these rules, and one draw needn't show every extreme that they name: `pixel_counts`: multiples of 4; some cycle has exactly 16384 pixels; pixel slots at or past a cycle's count are not used. `low_orders`: all distinct. `sky_mask`: Positive.
All inputs are finite; a program needn't handle non-finite values.
Results may differ from a plain program's by a relative error of at most 0.0046.
Values may be sent and summed in bfloat16 or wider, within the bound.
A program may use at most 128 MiB of HBM per device.

v0:
```python
import jax
import jax.numpy as jnp
from jax import lax
from jax.sharding import PartitionSpec as P


def slot_orders(low_orders, degree_count):
    return jnp.stack([low_orders, degree_count - low_orders], axis=1).reshape(-1)


def finish_cycle(pixel_sums, cycle_count, orders):
    slots = orders.shape[0]
    maps_count = pixel_sums.shape[1] // 2
    inverse_root = 1.0 / jnp.sqrt(cycle_count.astype(jnp.float32))
    real_part = (pixel_sums[:slots] * inverse_root).reshape(slots, 2, maps_count)
    imag_part = (-pixel_sums[slots:] * inverse_root).reshape(slots, 2, maps_count)
    joined = jnp.stack(
        [real_part[:, 0], imag_part[:, 0], real_part[:, 1], imag_part[:, 1]], axis=1
    ).reshape(slots, 4 * maps_count)
    live_slots = 2 * orders < cycle_count
    return jnp.where(live_slots[:, None], joined, 0.0).astype(jnp.bfloat16)


def cycle_fourier(cycle_maps, cycle_mask, cycle_count, cycle_offset, orders):
    maps_count = cycle_maps.shape[1]
    pixel_slots = cycle_maps.shape[2]
    cycle_rows = cycle_maps.reshape(2 * maps_count, pixel_slots)
    block_width = min(2048, pixel_slots)
    group_count = block_width // 128
    slots = orders.shape[0]
    modulus = 2 * cycle_count
    scale = jnp.pi / cycle_count.astype(jnp.float32)
    order_mod = orders % modulus
    fine_units = 2 * order_mod[:, None] * jnp.arange(128, dtype=jnp.int32)[None, :] % modulus
    fine_angle = scale * fine_units.astype(jnp.float32)
    fine_cos = jnp.cos(fine_angle)[:, None, :]
    fine_sin = jnp.sin(fine_angle)[:, None, :]

    def add_block(block_index, totals):
        first_pixel = block_index * block_width
        row_block = lax.dynamic_slice_in_dim(cycle_rows, first_pixel, block_width, 1)
        mask_block = lax.dynamic_slice_in_dim(cycle_mask, first_pixel, block_width, 0)
        pixels = first_pixel + jnp.arange(block_width, dtype=jnp.int32)
        masked = jnp.where(
            pixels[None, :] < cycle_count, mask_block[None, :] * row_block.astype(jnp.float32), 0.0
        ).astype(jnp.bfloat16)
        group_starts = first_pixel + 128 * jnp.arange(group_count, dtype=jnp.int32)
        coarse_units = (
            order_mod[:, None] * ((2 * group_starts[None, :] + cycle_offset) % modulus) % modulus
        )
        coarse_angle = scale * coarse_units.astype(jnp.float32)
        coarse_cos = jnp.cos(coarse_angle)[:, :, None]
        coarse_sin = jnp.sin(coarse_angle)[:, :, None]
        cosines = (coarse_cos * fine_cos - coarse_sin * fine_sin).reshape(slots, block_width)
        sines = (coarse_sin * fine_cos + coarse_cos * fine_sin).reshape(slots, block_width)
        tables = jnp.concatenate([cosines.astype(jnp.bfloat16), sines.astype(jnp.bfloat16)], axis=0)
        return totals + lax.dot_general(
            tables, masked, (((1,), (1,)), ((), ())), preferred_element_type=jnp.float32
        )

    block_count = (cycle_count + block_width - 1) // block_width
    pixel_sums = lax.fori_loop(
        0, block_count, add_block, jnp.zeros((2 * slots, 2 * maps_count), jnp.float32)
    )
    return finish_cycle(pixel_sums, cycle_count, orders)


def stacked_operand(block_rows):
    quarter = block_rows.shape[1] // 4
    q_real = block_rows[:, :quarter]
    q_imag = block_rows[:, quarter : 2 * quarter]
    u_real = block_rows[:, 2 * quarter : 3 * quarter]
    u_imag = block_rows[:, 3 * quarter :]
    lower_half = jnp.concatenate([u_imag, -u_real, -q_imag, q_real], axis=1)
    return jnp.concatenate([block_rows, lower_half], axis=0)


def pair_alm(legendre_rows, first_order, first_block, second_block):
    first_operand = stacked_operand(first_block)
    second_operand = stacked_operand(second_block)
    degree_count, inner_width = legendre_rows.shape
    tile_height = min(128, degree_count)
    tile_count = degree_count // tile_height
    split_row = degree_count - first_order
    tile_starts = jnp.arange(tile_count, dtype=jnp.int32) * tile_height
    chosen = jnp.where(
        (tile_starts < split_row)[:, None, None], first_operand[None], second_operand[None]
    )
    tile_product = jnp.einsum(
        "tir,tro->tio",
        legendre_rows.reshape(tile_count, tile_height, inner_width),
        chosen,
        preferred_element_type=jnp.float32,
    )
    tile_product = tile_product.reshape(degree_count, first_operand.shape[1])
    border = split_row // tile_height * tile_height
    border_rows = lax.dynamic_slice_in_dim(legendre_rows, border, tile_height, 0)
    border_product = jnp.dot(border_rows, second_operand, preferred_element_type=jnp.float32)
    current = lax.dynamic_slice_in_dim(tile_product, border, tile_height, 0)
    row_index = border + jnp.arange(tile_height, dtype=jnp.int32)
    patched = jnp.where((row_index >= split_row)[:, None], border_product, current)
    return -lax.dynamic_update_slice_in_dim(tile_product, patched, border, 0)


def dense_pair(alm_rows, first_order):
    degree_count = alm_rows.shape[0]
    degrees = jnp.arange(degree_count, dtype=jnp.int32)
    first_dense = jnp.where(
        (degrees >= first_order)[:, None], jnp.roll(alm_rows, first_order, axis=0), 0.0
    ).astype(jnp.bfloat16)
    second_dense = jnp.where(
        (degrees >= degree_count - first_order)[:, None], alm_rows, 0.0
    ).astype(jnp.bfloat16)
    return jnp.stack([first_dense, second_dense], axis=0)


def outer_totals(rows, maps_count):
    split_parts = rows.reshape(rows.shape[0], rows.shape[1], 2, 2, maps_count)
    return jnp.einsum(
        "slerm,slern->lemn", split_parts, split_parts, preferred_element_type=jnp.float32
    )


def scaled_spectra(totals, degrees, orders, weight, maps_count):
    counts = jnp.maximum(
        jnp.sum((orders[None, :] <= degrees[:, None]).astype(jnp.int32), axis=1), 1
    ).astype(jnp.float32)
    return (2.0 * totals / (weight * counts)[:, None, None, None]).reshape(
        degrees.shape[0], 2, maps_count * maps_count
    )


def local(sky_maps, sky_mask, pixel_counts, phi_offsets, low_orders, legendre):
    devices = lax.axis_size(("band", "sub"))
    device_index = lax.axis_index(("band", "sub"))
    degree_count = legendre.shape[1]
    orders = slot_orders(low_orders, degree_count)
    cycle_local = sky_maps.shape[0]
    maps_count = sky_maps.shape[2]
    pair_local = legendre.shape[0]
    slot_local = 2 * pair_local
    columns = 4 * maps_count
    valid_pixels = jnp.arange(sky_maps.shape[3], dtype=jnp.int32)[None, :] < pixel_counts[:, None]
    local_square = jnp.sum(jnp.where(valid_pixels, sky_mask * sky_mask, 0.0))
    local_pixels = jnp.sum(pixel_counts.astype(jnp.float32))
    total_square, total_pixels = lax.psum((local_square, local_pixels), ("band", "sub"))
    weight = total_square / total_pixels
    cycle_blocks = [
        cycle_fourier(sky_maps[0], sky_mask[0], pixel_counts[0], phi_offsets[0], orders)
    ]
    coefficients = jnp.stack(cycle_blocks, axis=1).reshape(
        devices, slot_local, cycle_local, columns
    )
    received = lax.all_to_all(
        coefficients, ("band", "sub"), split_axis=0, concat_axis=0, tiled=True
    )
    cycle_total = devices * cycle_local
    first_order = lax.dynamic_index_in_dim(
        low_orders, device_index * pair_local + 0, 0, keepdims=False
    )
    first_block = received[:, 0].reshape(cycle_total, columns)
    second_block = received[:, 1].reshape(cycle_total, columns)
    alm_pairs = [pair_alm(legendre[0], first_order, first_block, second_block)]
    alm_packed = jnp.stack(alm_pairs, axis=0)
    dense_local = dense_pair(alm_pairs[0], first_order)
    by_degree = lax.all_to_all(
        dense_local, ("band", "sub"), split_axis=1, concat_axis=0, tiled=True
    )
    degree_local = by_degree.shape[1]
    degrees = device_index * degree_local + jnp.arange(degree_local, dtype=jnp.int32)
    totals = outer_totals(by_degree, maps_count)
    spectra = scaled_spectra(totals, degrees, orders, weight, maps_count)
    return (alm_packed, spectra)


def solution(mesh):
    placed = (
        P(("groups", "band", "sub"), None, None, None),
        P(("groups", "band", "sub"), None),
        P(("groups", "band", "sub")),
        P(("groups", "band", "sub")),
        P("groups"),
        P(("groups", "band", "sub"), None, None),
    )
    return jax.shard_map(
        local,
        mesh=mesh,
        in_specs=placed,
        out_specs=(
            P(("groups", "band", "sub"), None, None),
            P(("groups", "band", "sub"), None, None),
        ),
        check_vma=False,
    )
```

profile of v0, /device:TPU:18, one launch (start us, length us, event | category | flops | bytes accessed | tf_op | source)
XLA Modules:
  0.0 301.1 jit_solution(14685588854479680032)
XLA Ops:
  1.4 0.7 subtract_bitcast_fusion
  2.0 0.7 pad_add_fusion
  3.1 26.0 %while.14 = (s32[]{:T(128)}, f32[64,64]{1,0:T(8,128)S(1)}, s32[]{:T(128)}, f32[]{:T(128)}, s32[32]{0:T(128)S(1)}, /*index=5*/s32[]{:T(128)}, s32[]{:T(128)}, pre...) while((s32[]{:T(128)}, f32[64,64]{1,0:T(8,128)S(1)}, ...), condition=%wide.region_1.2_spmd.clone.clone, body=%wide.region_0.1_spmd.clone.clone.sunk | while | flops 18404532 | bytes 1446522 | solution.py:62
  3.1 0.4 cosine_bitcast_fusion.2
  3.4 0.8 and_select_fusion.4
  4.2 0.4 fusion.55
  4.8 0.7 dynamic_slice.63
  5.5 0.7 add_compare_fusion.3
  6.2 1.2 convolution_add_fusion.2
  7.4 0.4 cosine_bitcast_fusion.2
  7.8 0.8 and_select_fusion.4
  8.5 0.4 fusion.55
  8.9 0.2 subtract_convert_fusion.2
  9.2 0.7 dynamic_slice.63
  9.9 0.7 add_compare_fusion.3
  10.5 1.2 convolution_add_fusion.2
  11.7 0.4 cosine_bitcast_fusion.2
  12.1 0.8 and_select_fusion.4
  12.9 0.4 fusion.55
  13.2 0.2 subtract_convert_fusion.2
  13.5 0.7 dynamic_slice.63
  14.2 0.7 add_compare_fusion.3
  14.9 1.2 convolution_add_fusion.2
  16.1 0.4 cosine_bitcast_fusion.2
  16.4 0.8 and_select_fusion.4
  17.2 0.4 fusion.55
  17.6 0.2 subtract_convert_fusion.2
  17.8 0.7 dynamic_slice.63
  18.5 0.7 add_compare_fusion.3
  19.2 1.2 convolution_add_fusion.2
  20.4 0.4 cosine_bitcast_fusion.2
  20.8 0.8 and_select_fusion.4
  21.5 0.4 fusion.55
  21.9 0.2 subtract_convert_fusion.2
  22.2 0.7 dynamic_slice.63
  22.9 0.7 add_compare_fusion.3
  23.5 1.2 convolution_add_fusion.2
  24.7 0.4 cosine_bitcast_fusion.2
  25.1 0.8 and_select_fusion.4
  25.9 0.4 fusion.55
  26.2 0.2 subtract_convert_fusion.2
  26.5 0.7 dynamic_slice.63
  27.2 0.7 add_compare_fusion.3
  27.9 1.2 convolution_add_fusion.2
  29.6 0.7 select_convert_fusion.3
  30.3 13.3 %all-to-all-start = ((bf16[16,2,1,128]{3,1,2,0:T(2,128)(2,1)}), bf16[16,2,1,128]{3,1,2,0:T(2,128)(2,1)S(1)}, u32[]{:S(2)}, u32[]{:S(2)}) async-start(bf16[16,2,1,128]{3,1,2,0:T(2,128)(2,1)} %select_convert_fusion.3), calls=%async_computation | async-start | bytes 16384 | tf_op jit(solution)/shard_map/all_to_all | solution.py:154
  43.6 0.6 dynamic_slice.26
  44.8 0.7 iota_compare_fusion.1
  48.0 0.9 fusion.34
  49.1 0.2 neg.23
  49.3 5.4 %fusion.31 = (bf16[1,8192,128]{2,1,0:T(8,128)(2,1)S(1)}, f32[1,8192,128]{2,1,0:T(8,128)}) fusion(pred[8192]{0:T(1024)(128)(4,1)S(1)} %iota_compare_fusion, f32[8192,128]{1,0:T(8,128)S(1)} %fusion.33), kind=kLoop, calls=%fused_computation.49 | loop fusion | flops 3145728 | bytes 10493952 | tf_op jit(solution)/shard_map/stack | solution.py:114
  54.7 11.8 %fusion.32 = bf16[1,8192,128]{2,1,0:T(8,128)(2,1)S(1)} fusion(s32[]{:T(128)S(6)} %select_n.144, bf16[8192,128]{1,0:T(8,128)(2,1)S(1)} %neg.23, pred[8192]{0:T(1024)(128)(4,1)S(1)} %iota_compare_fusion.1), kind=kLoop, calls=%fused_computation.50 | loop fusion | flops 5242880 | bytes 4202500 | tf_op jit(solution)/shard_map/stack | solution.py:114
  66.5 0.4 pad_maximum_fusion
  66.9 35.4 %copy.69 = bf16[2,8192,128]{2,0,1:T(2,128)(2,1)} copy(bf16[2,8192,128]{2,1,0:T(8,128)(2,1)S(1)} %pad_maximum_fusion) | data formatting | bytes 8388608 | tf_op jit(solution)/shard_map/stack | solution.py:114
  102.3 6.8 %all-to-all-start.1 = ((bf16[2,8192,128]{2,0,1:T(2,128)(2,1)}), bf16[2,8192,128]{2,0,1:T(2,128)(2,1)}, u32[]{:S(2)}, u32[]{:S(2)}) async-start(bf16[2,8192,128]{2,0,1:T(2,128)(2,1)} %copy.69), calls=%async_computation.1 | async-start | bytes 8388608 | tf_op jit(solution)/shard_map/all_to_all | solution.py:166
  109.2 0.8 fusion.40
  110.0 110.5 %all-reduce = (f32[]{:T(128)}, f32[]{:T(128)}) all-reduce(f32[]{:T(128)} %fusion.40, f32[]{:T(128)} %bitcast.21), channel_id=1, replica_groups=mesh['groups'=2,'band'=8,'sub'=2] {'band','sub'}, use_global_device_ids=true, to_apply=%region_3.4 | all-reduce | flops 2 | bytes 16 | tf_op jit(solution)/shard_map/psum | solution.py:146
  221.9 4.7 %copy.70 = bf16[2,8192,128]{2,1,0:T(8,128)(2,1)} copy(bf16[2,8192,128]{2,0,1:T(2,128)(2,1)} %all-to-all-done.1) | data formatting | bytes 8388608 | tf_op jit(solution)/shard_map/all_to_all | solution.py:166
  226.6 6.4 %copy.71 = bf16[16,2,512,128]{2,3,1,0:T(8,128)(2,1)} copy(bf16[16,2,512,128]{3,2,0,1:T(8,128)(2,1)} %bitcast.69) | data formatting | bytes 8388608 | tf_op jit(solution)/shard_map/all_to_all | solution.py:166
  233.0 23.2 %copy.73 = bf16[32,512,2,2,32]{4,0,3,2,1:T(8,128)(2,1)} copy(bf16[32,512,2,2,32]{1,4,3,2,0:T(8,128)(2,1)} %bitcast.67) | data formatting | bytes 8388608 | tf_op jit(solution)/shard_map/reshape | solution.py:118
  256.3 21.0 %convolution_bitcast_fusion = f32[512,2,32,32]{3,2,1,0:T(8,128)} fusion(bf16[32,512,2,2,32]{4,0,3,2,1:T(8,128)(2,1)} %copy.73), kind=kOutput, calls=%fused_computation.40 | convolution fusion | flops 134217728 | bytes 8388608 | tf_op jit(solution)/shard_map/slerm,slern->lemn/dot_general | solution.py:119
  277.3 11.4 %copy.74 = f32[512,2,32,32]{0,3,2,1:T(8,128)} copy(f32[512,2,32,32]{3,2,1,0:T(8,128)} %convolution_bitcast_fusion) | data formatting | bytes 8388608 | tf_op jit(solution)/shard_map/slerm,slern->lemn/dot_general | solution.py:119
  288.7 5.1 %multiply_divide_fusion = f32[512,2,32,32]{0,3,2,1:T(8,128)} fusion(f32[512,2,32,32]{0,3,2,1:T(8,128)} %copy.74, f32[512]{0:T(512)S(1)} %convert_multiply_fusion), kind=kLoop, calls=%fused_computation.47 | loop fusion | flops 2097152 | bytes 8390656 | tf_op jit(solution)/shard_map/div | solution.py:128
  293.8 7.3 %copy.75 = f32[512,2,1024]{2,1,0:T(2,128)} copy(f32[512,2,1024]{0,2,1:T(8,128)} %bitcast.68) | data formatting | bytes 8388608
  (42 shorter events, 2.2 us)
Async XLA Ops:
  3.0 26.5 %copy-start.2 = (s32[16]{0:T(128)S(1)}, s32[16]{0:T(128)}, u32[]{:S(2)}) copy-start(s32[16]{0:T(128)} %param.12) | copy-start | bytes 196
  3.0 44.4 %copy-start = (bf16[1,8192,32]{1,2,0:T(8,128)(2,1)S(1)}, bf16[1,8192,32]{1,2,0:T(8,128)(2,1)}, u32[]{:S(2)}) copy-start(bf16[1,8192,32]{1,2,0:T(8,128)(2,1)} %param.13) | copy-start | bytes 1572868
  30.3 17.4 %all-to-all-start = ((bf16[16,2,1,128]{3,1,2,0:T(2,128)(2,1)}), bf16[16,2,1,128]{3,1,2,0:T(2,128)(2,1)S(1)}, u32[]{:S(2)}, u32[]{:S(2)}) async-start(bf16[16,2,1,128]{3,1,2,0:T(2,128)(2,1)} %select_convert_fusion.3), calls=%async_computation | async-start | bytes 16384 | tf_op jit(solution)/shard_map/all_to_all | solution.py:154
  102.3 6.8 %copy-start.1 = (f32[16384]{0:T(1024)S(1)}, f32[16384]{0:T(1024)}, u32[]{:S(2)}) copy-start(f32[16384]{0:T(1024)} %get-tuple-element.441) | copy-start | bytes 196612
  102.3 119.5 %all-to-all-start.1 = ((bf16[2,8192,128]{2,0,1:T(2,128)(2,1)}), bf16[2,8192,128]{2,0,1:T(2,128)(2,1)}, u32[]{:S(2)}, u32[]{:S(2)}) async-start(bf16[2,8192,128]{2,0,1:T(2,128)(2,1)} %copy.69), calls=%async_computation.1 | async-start | bytes 8388608 | tf_op jit(solution)/shard_map/all_to_all | solution.py:166
where the time goes:
time: 303 us; the launch traced here: 301 us
  blocking collectives  111 us (37%)
  local copies, waits for them, and re-layouts  94.4 us (31%)
  other arithmetic  41.1 us (14%)
  matrix products  29.1 us (10%)
  starting transfers between devices  20.1 us (7%)
  between operations  5.55 us (2%)
    psum x1, blocking collectives, local(): lax.psum((local_square, local_pixels), ('band', 'sub'))  111 us
    another operation x1, local copies, waits for them, and re-layouts, dense_pair(): return jnp.stack([first_dense, second_dense], axis=0)  35.4 us
    reshape x1, local copies, waits for them, and re-layouts, outer_totals(): split_parts = rows.reshape(rows.shape[0], rows.shape[1], 2, 2, maps_count)  23.2 us
    dot_general x1, matrix products, outer_totals(): jnp.einsum('slerm,slern->lemn', split_parts, split_parts, preferred_eleme...  21 us
    another operation x3, other arithmetic, dense_pair(): return jnp.stack([first_dense, second_dense], axis=0)  17.6 us
    all_to_all x1, starting transfers between devices, local(): lax.all_to_all(coefficients, ('band', 'sub'), split_axis=0, concat_axis=0...  13.3 us
    dot_general x1, local copies, waits for them, and re-layouts, outer_totals(): jnp.einsum('slerm,slern->lemn', split_parts, split_parts, preferred_eleme...  11.4 us
    all_to_all x2, local copies, waits for them, and re-layouts, local(): lax.all_to_all(dense_local, ('band', 'sub'), split_axis=1, concat_axis=0,...  11.2 us
  transfers between devices with their start and end apart: 2, of which 0 were waited for; matrix products, arithmetic and copies ran while one was open for 1% of the time, Pallas kernels for 0%

commit v1 on v0

--- a/solution.py
+++ b/solution.py
@@ -1,6 +1,10 @@
+import functools
+
 import jax
 import jax.numpy as jnp
 from jax import lax
+from jax.experimental import pallas as pl
+from jax.experimental.pallas import tpu as pltpu
 from jax.sharding import PartitionSpec as P
 
 
@@ -130,7 +134,342 @@
     )
 
 
-def local(sky_maps, sky_mask, pixel_counts, phi_offsets, low_orders, legendre):
+EXTRA = 16
+
+
+def fourier_kernel(maps_ref, mask_ref, fine_ref, coarse_ref, live_ref, out_ref, total):
+    step = pl.program_id(0)
+    slots = fine_ref.shape[1]
+    groups = maps_ref.shape[1] // 128
+    fine_cos = fine_ref[0]
+    fine_sin = fine_ref[1]
+    cosines = []
+    sines = []
+    for group in range(groups):
+        coarse_cos = coarse_ref[0, 0, :, group : group + 1]
+        coarse_sin = coarse_ref[1, 0, :, group : group + 1]
+        cosines.append((coarse_cos * fine_cos - coarse_sin * fine_sin).astype(jnp.bfloat16))
+        sines.append((coarse_sin * fine_cos + coarse_cos * fine_sin).astype(jnp.bfloat16))
+    tables = jnp.concatenate(
+        [jnp.concatenate(cosines, axis=1), jnp.concatenate(sines, axis=1)], axis=0
+    )
+    masked = (maps_ref[...].astype(jnp.float32) * mask_ref[...]).astype(jnp.bfloat16)
+    sums = lax.dot_general(
+        tables, masked, (((1,), (1,)), ((), ())), preferred_element_type=jnp.float32
+    )
+
+    @pl.when(step == 0)
+    def _():
+        total[...] = sums
+
+    @pl.when(step > 0)
+    def _():
+        total[...] += sums
+
+    @pl.when(step == pl.num_programs(0) - 1)
+    def _():
+        half = maps_ref.shape[0] // 2
+        real = total[:slots]
+        imag = -total[slots:]
+        joined = jnp.concatenate(
+            [real[:, :half], imag[:, :half], real[:, half:], imag[:, half:]], axis=1
+        )
+        out_ref[...] = (joined * live_ref[...]).astype(jnp.bfloat16)
+
+
+def fourier_call(cycle_maps, masked_weight, cycle_count, cycle_offset, orders):
+    maps_count = cycle_maps.shape[1]
+    pixel_slots = cycle_maps.shape[2]
+    rows = cycle_maps.reshape(2 * maps_count, pixel_slots)
+    slots = orders.shape[0]
+    width = min(2048, pixel_slots)
+    blocks = pixel_slots // width
+    groups = width // 128
+    modulus = 2 * cycle_count
+    scale = jnp.pi / cycle_count.astype(jnp.float32)
+    order_mod = orders % modulus
+    fine_units = 2 * order_mod[:, None] * jnp.arange(128, dtype=jnp.int32)[None, :] % modulus
+    starts = 128 * jnp.arange(blocks * groups, dtype=jnp.int32)
+    starts = ((2 * starts + cycle_offset) % modulus).reshape(blocks, 1, groups)
+    coarse_units = order_mod[None, :, None] * starts % modulus
+    fine_angle = scale * fine_units.astype(jnp.float32)
+    coarse_angle = scale * coarse_units.astype(jnp.float32)
+    fine = jnp.stack([jnp.cos(fine_angle), jnp.sin(fine_angle)])
+    coarse = jnp.stack([jnp.cos(coarse_angle), jnp.sin(coarse_angle)])
+    inverse_root = 1.0 / jnp.sqrt(cycle_count.astype(jnp.float32))
+    live = jnp.broadcast_to(
+        jnp.where(2 * orders < cycle_count, inverse_root, 0.0)[:, None], (slots, 4 * maps_count)
+    )
+    return pl.pallas_call(
+        fourier_kernel,
+        grid=(blocks,),
+        in_specs=[
+            pl.BlockSpec((2 * maps_count, width), lambda i: (0, i)),
+            pl.BlockSpec((1, width), lambda i: (0, i)),
+            pl.BlockSpec((2, slots, 128), lambda i: (0, 0, 0)),
+            pl.BlockSpec((2, 1, slots, groups), lambda i: (0, i, 0, 0)),
+            pl.BlockSpec((slots, 4 * maps_count), lambda i: (0, 0)),
+        ],
+        out_specs=pl.BlockSpec((slots, 4 * maps_count), lambda i: (0, 0)),
+        out_shape=jax.ShapeDtypeStruct((slots, 4 * maps_count), jnp.bfloat16),
+        scratch_shapes=[pltpu.VMEM((2 * slots, 2 * maps_count), jnp.float32)],
+        cost_estimate=pl.CostEstimate(
+            flops=8 * slots * maps_count * pixel_slots,
+            bytes_accessed=4 * maps_count * pixel_slots,
+            transcendentals=0,
+        ),
+    )(rows, masked_weight, fine, coarse, live)
+
+
+def operand_rows(wide, slot, cycles, stride):
+    upper = wide[pl.ds(slot, cycles, stride=stride), :]
+    quarter = upper.shape[1] // 4
+    lower = jnp.concatenate(
+        [
+            upper[:, 3 * quarter :],
+            -upper[:, 2 * quarter : 3 * quarter],
+            -upper[:, quarter : 2 * quarter],
+            upper[:, :quarter],
+        ],
+        axis=1,
+    )
+    return jnp.concatenate([upper, lower], axis=0)
+
+
+def alm_kernel(stride, scalar_ref, gathered_ref, legendre_ref, out_ref, wide, operand):
+    step = pl.program_id(0)
+    height = out_ref.shape[0]
+    columns = out_ref.shape[1]
+    cycles = gathered_ref.shape[0] // stride
+
+    @pl.when(step == 0)
+    def _():
+        wide[...] = gathered_ref[...].astype(jnp.float32)
+        pair = scalar_ref[0]
+        operand[...] = -jnp.concatenate(
+            [
+                operand_rows(wide, 2 * pair, cycles, stride),
+                operand_rows(wide, 2 * pair + 1, cycles, stride),
+            ],
+            axis=1,
+        )
+
+    product = lax.dot_general(
+        legendre_ref[...],
+        operand[...].astype(jnp.bfloat16),
+        (((0,), (0,)), ((), ())),
+        preferred_element_type=jnp.float32,
+    )
+    row = step * height + lax.broadcasted_iota(jnp.int32, (height, columns), 0)
+    out_ref[...] = jnp.where(row < scalar_ref[1], product[:, :columns], product[:, columns:])
+
+
+def alm_call(scalars, gathered, stride, legendre_cols):
+    inner, degree_count = legendre_cols.shape
+    columns = gathered.shape[1]
+    height = min(1024, degree_count)
+    return pl.pallas_call(
+        functools.partial(alm_kernel, stride),
+        grid=(degree_count // height,),
+        in_specs=[
+            pl.BlockSpec(memory_space=pltpu.SMEM),
+            pl.BlockSpec(gathered.shape, lambda i: (0, 0)),
+            pl.BlockSpec((inner, height), lambda i: (0, i)),
+        ],
+        out_specs=pl.BlockSpec((height, columns), lambda i: (i, 0)),
+        out_shape=jax.ShapeDtypeStruct((degree_count, columns), jnp.float32),
+        scratch_shapes=[
+            pltpu.VMEM(gathered.shape, jnp.float32),
+            pltpu.VMEM((inner, 2 * columns), jnp.float32),
+        ],
+        cost_estimate=pl.CostEstimate(
+            flops=4 * degree_count * inner * columns,
+            bytes_accessed=4 * degree_count * columns,
+            transcendentals=0,
+        ),
+    )(scalars, gathered, legendre_cols)
+
+
+def spectra_kernel(stride, scale_ref, gathered_ref, legendre_ref, out_ref, wide, operands, dense, turned):
+    step = pl.program_id(0)
+    cycles = gathered_ref.shape[0] // stride
+    inner = 2 * cycles
+    slots = legendre_ref.shape[0] // inner
+    height = legendre_ref.shape[1]
+    per_group = 128 // inner
+    group_count = slots // per_group
+
+    @pl.when(step == 0)
+    def _():
+        wide[...] = gathered_ref[...].astype(jnp.float32)
+        for slot in range(slots):
+            operands[slot * inner : (slot + 1) * inner, :] = operand_rows(
+                wide, slot, cycles, stride
+            ).astype(jnp.bfloat16)
+
+    def spread(tall, piece):
+        parts = []
+        for index in range(128 // piece):
+            own = tall[index * piece : (index + 1) * piece]
+            column = []
+            if index > 0:
+                column.append(jnp.zeros((index * piece, 128), tall.dtype))
+            column.append(own)
+            if (index + 1) * piece < 128:
+                column.append(jnp.zeros((128 - (index + 1) * piece, 128), tall.dtype))
+            parts.append(jnp.concatenate(column, axis=0))
+        return jnp.concatenate(parts, axis=1)
+
+    for group in range(group_count):
+        wide_operand = spread(operands[group * 128 : (group + 1) * 128, :], inner)
+        product = lax.dot_general(
+            legendre_ref[group * 128 : (group + 1) * 128, :],
+            wide_operand,
+            (((0,), (0,)), ((), ())),
+            preferred_element_type=jnp.float32,
+        )
+        for index in range(per_group):
+            dense[pl.ds(group * per_group + index, height, stride=slots), :] = product[
+                :, index * 128 : (index + 1) * 128
+            ]
+
+    per_batch = 128 // slots
+    lane_group = lax.broadcasted_iota(jnp.int32, (8, 128), 1) // 32
+
+    def batch(position, carry):
+        rows = dense[pl.ds(pl.multiple_of(position * 128, 128), 128), :]
+        turned[...] = rows.T
+        left = jnp.concatenate(
+            [
+                turned[pl.ds(32 * part + quarter, 8, stride=4), :]
+                for part in range(4)
+                for quarter in range(4)
+            ],
+            axis=0,
+        ).astype(jnp.bfloat16)
+        gram = jnp.dot(
+            left, spread(rows.astype(jnp.bfloat16), slots), preferred_element_type=jnp.float32
+        )
+        for index in range(per_batch):
+            degree = position * per_batch + index
+            factor = scale_ref[step * height + degree]
+            for kind in range(2):
+                result = None
+                for turn in range(4):
+                    first = 32 * (2 * kind) + 8 * ((2 * kind + turn) % 4)
+                    second = 32 * (2 * kind + 1) + 8 * ((2 * kind + 1 + turn) % 4)
+                    lanes = slice(index * 128, (index + 1) * 128)
+                    value = jnp.where(
+                        lane_group == 2 * kind,
+                        gram[first : first + 8, lanes],
+                        jnp.where(
+                            lane_group == 2 * kind + 1, gram[second : second + 8, lanes], 0.0
+                        ),
+                    )
+                    if turn > 0:
+                        value = pltpu.roll(value, 32 * turn, axis=1)
+                    result = value if result is None else result + value
+                out_ref[pl.ds(degree * 16 + kind, 8, stride=2), :] = result * factor
+        return carry
+
+    lax.fori_loop(0, height // per_batch, batch, 0, unroll=2)
+
+
+def spectra_call(scale, gathered, stride, legendre_rows):
+    row_count, degree_local = legendre_rows.shape
+    columns = gathered.shape[1]
+    inner = 2 * (gathered.shape[0] // stride)
+    slots = row_count // inner
+    height = 128
+    result = pl.pallas_call(
+        functools.partial(spectra_kernel, stride),
+        grid=(degree_local // height,),
+        in_specs=[
+            pl.BlockSpec(memory_space=pltpu.SMEM),
+            pl.BlockSpec(gathered.shape, lambda i: (0, 0)),
+            pl.BlockSpec((row_count, height), lambda i: (0, i)),
+        ],
+        out_specs=pl.BlockSpec((height * 16, 128), lambda i: (i, 0)),
+        out_shape=jax.ShapeDtypeStruct((degree_local * 16, 128), jnp.float32),
+        scratch_shapes=[
+            pltpu.VMEM(gathered.shape, jnp.float32),
+            pltpu.VMEM((row_count, columns), jnp.bfloat16),
+            pltpu.VMEM((height * slots, columns), jnp.float32),
+            pltpu.VMEM((128, 128), jnp.float32),
+        ],
+        cost_estimate=pl.CostEstimate(
+            flops=degree_local * slots * 4 * columns * columns,
+            bytes_accessed=4 * degree_local * 2048,
+            transcendentals=0,
+        ),
+    )(scale, gathered, legendre_rows)
+    return (
+        result.reshape(degree_local, 8, 2, 128)
+        .transpose(0, 2, 1, 3)
+        .reshape(degree_local, 2, 1024)
+    )
+
+
+def split_three(value):
+    pieces = []
+    rest = value
+    for _ in range(3):
+        piece = lax.reduce_precision(rest, 8, 7)
+        pieces.append(piece)
+        rest = rest - piece
+    return pieces
+
+
+def compact(sky_maps, sky_mask, pixel_counts, phi_offsets, low_orders, legendre):
+    axes = ("band", "sub")
+    devices = lax.axis_size(axes)
+    device_index = lax.axis_index(axes)
+    degree_count = legendre.shape[1]
+    inner = legendre.shape[2]
+    slots = 2 * low_orders.shape[0]
+    orders = slot_orders(low_orders, degree_count)
+    degree_local = degree_count // devices
+    first_order = lax.dynamic_index_in_dim(low_orders, device_index, 0, keepdims=False)
+    split_row = degree_count - first_order
+    legendre_cols = legendre[0].T
+    degrees = jnp.arange(degree_count, dtype=jnp.int32)[None, :]
+    doubled = jnp.concatenate([legendre_cols, legendre_cols], axis=1)
+    rolled = lax.dynamic_slice_in_dim(doubled, split_row, degree_count, 1)
+    first = jnp.where(degrees >= first_order, rolled, 0.0).astype(jnp.bfloat16)
+    second = jnp.where(degrees >= split_row, legendre_cols, 0.0).astype(jnp.bfloat16)
+    sent = jnp.concatenate([first, second], axis=0)
+    sent = sent.reshape(2 * inner, devices, degree_local).transpose(1, 0, 2)
+    received = lax.all_to_all(sent, axes, split_axis=0, concat_axis=0, tiled=True)
+    legendre_rows = received.reshape(slots * inner, degree_local)
+
+    count = pixel_counts[0]
+    valid = jnp.arange(sky_mask.shape[1], dtype=jnp.int32)[None, :] < count
+    masked_weight = jnp.where(valid, sky_mask, 0.0)
+    coefficients = fourier_call(sky_maps[0], masked_weight, count, phi_offsets[0], orders)
+    square = split_three(jnp.sum(masked_weight * masked_weight))
+    pixels = split_three(count.astype(jnp.float32))
+    columns = coefficients.shape[1]
+    extra = jnp.zeros((EXTRA, columns), jnp.float32)
+    column_index = lax.broadcasted_iota(jnp.int32, (EXTRA, columns), 1)
+    for index, piece in enumerate(square + pixels):
+        extra = jnp.where(column_index == index, piece, extra)
+    payload = jnp.concatenate([coefficients, extra.astype(jnp.bfloat16)], axis=0)
+    gathered = lax.all_gather(payload, axes, axis=0, tiled=True)
+    stride = slots + EXTRA
+    pieces = gathered.reshape(devices, stride, columns)[:, slots, :6].astype(jnp.float32)
+    weight = jnp.sum(pieces[:, :3]) / jnp.sum(pieces[:, 3:])
+    scalars = jnp.stack([device_index.astype(jnp.int32), split_row])
+    alm_packed = alm_call(scalars, gathered, stride, legendre_cols)
+    own = device_index * degree_local + jnp.arange(degree_local, dtype=jnp.int32)
+    counts = jnp.maximum(
+        jnp.sum((orders[None, :] <= own[:, None]).astype(jnp.int32), axis=1), 1
+    ).astype(jnp.float32)
+    scale = 2.0 / (weight * counts)
+    spectra = spectra_call(scale, gathered, stride, legendre_rows)
+    return (alm_packed[None], spectra)
+
+
+def general(sky_maps, sky_mask, pixel_counts, phi_offsets, low_orders, legendre):
     devices = lax.axis_size(("band", "sub"))
     device_index = lax.axis_index(("band", "sub"))
     degree_count = legendre.shape[1]
@@ -173,6 +512,23 @@
     return (alm_packed, spectra)
 
 
+def local(sky_maps, sky_mask, pixel_counts, phi_offsets, low_orders, legendre):
+    devices = lax.axis_size(("band", "sub"))
+    fits = (
+        sky_maps.shape[0] == 1
+        and legendre.shape[0] == 1
+        and sky_maps.shape[2] == 32
+        and sky_maps.shape[3] % 2048 == 0
+        and 2 * low_orders.shape[0] in (16, 32, 64)
+        and legendre.shape[2] == 2 * devices
+        and legendre.shape[2] in (16, 32, 64)
+        and legendre.shape[1] % (128 * devices) == 0
+        and legendre.shape[1] % 1024 == 0
+    )
+    body = compact if fits else general
+    return body(sky_maps, sky_mask, pixel_counts, phi_offsets, low_orders, legendre)
+
+
 def solution(mesh):
     placed = (
         P(("groups", "band", "sub"), None, None, None),

time: 303 us -> 105 us (0.35)
  the two profiles are of different devices: /device:TPU:18 before, /device:TPU:0 now
where the time goes in v1:
time: 105 us; the launch traced here: 104 us
  Pallas kernels  44.6 us (42%)
  blocking collectives  22.2 us (21%)
  other arithmetic  14.1 us (13%)
  between operations  11.7 us (11%)
  starting transfers between devices  7.41 us (7%)
  local copies, waits for them, and re-layouts  4.24 us (4%)
    pallas_call x1, Pallas kernels, spectra_call(): pl.pallas_call(functools.partial(spectra_kernel, stride), grid=(degree_lo...  31.2 us
    all_gather x1, blocking collectives, compact(): gathered = lax.all_gather(payload, axes, axis=0, tiled=True)  22.2 us
    all_to_all x1, starting transfers between devices, compact(): lax.all_to_all(sent, axes, split_axis=0, concat_axis=0, tiled=True)  7.41 us
    pallas_call x1, Pallas kernels, alm_call(): pl.pallas_call(functools.partial(alm_kernel, stride), grid=(degree_count...  6.79 us
    pallas_call x1, Pallas kernels, fourier_call(): pl.pallas_call(fourier_kernel, grid=(blocks,), in_specs=[pl.BlockSpec((2...  6.62 us
    convert_element_type x1, other arithmetic, compact(): extra.astype(jnp.bfloat16)  3.09 us
  transfers between devices with their start and end apart: 1, of which 0 were waited for; matrix products, arithmetic and copies ran while one was open for 12% of the time, Pallas kernels for 13%

profile of v1, /device:TPU:0, one launch (start us, length us, event | category | flops | bytes accessed | tf_op | source)
XLA Modules:
  0.0 104.3 jit_solution(8434543030769965468)
XLA Ops:
  0.6 1.2 %dynamic_slice.7 = s32[1]{0:T(128)} dynamic-slice(s32[16]{0:T(128)} %param.10, s32[]{:T(128)S(6)} %select_n.107), dynamic_slice_sizes={1} | dynamic-slice | bytes 12 | tf_op jit(solution)/shard_map/jit(dynamic_index_in_dim)/dynamic_slice | solution.py:432
  1.9 0.7 iota_compare_fusion.1
  3.9 1.8 %fusion.1 = (bf16[32,8192]{1,0:T(8,128)(2,1)S(1)}, bf16[32,8192]{1,0:T(8,128)(2,1)S(1)}) fusion(s32[]{:T(128)S(6)} %select_n.121, bf16[32,8192]{1,0:T(8,128)(2,1)} %bitcast.36, pred[8192]{0:T(1024)(128)(4,1)S(1)} %iota_compare_fusion.1, bf16[1,8192,32]{1,2,0:T(8,128)(2,1)} %param.11, pred[8192]{0:T(1024)(128)(4,1)S(1)} %iota_compare_fusion), kind=kLoop, calls=%fused_computation.5 | loop fusion | flops 1572864 | bytes 2113540 | tf_op jit(solution)/shard_map/jit(_where)/select_n | solution.py:438
  5.7 0.1 pad_maximum_fusion
  5.8 0.0 copy-start.3
  5.8 0.0 copy-start.2
  5.8 1.1 %copy.23 = bf16[8,16,8,512]{3,2,0,1:T(8,128)(2,1)} copy(bf16[8,16,8,512]{3,2,1,0:T(8,128)(2,1)S(1)} %bitcast.41) | data formatting | bytes 2097152 | tf_op jit(solution)/shard_map/reshape | solution.py:441
  6.8 7.4 %all-to-all-start = ((bf16[16,64,512]{2,1,0:T(8,128)(2,1)}), bf16[16,64,512]{2,1,0:T(8,128)(2,1)S(1)}, u32[]{:S(2)}, u32[]{:S(2)}) async-start(bf16[16,64,512]{2,1,0:T(8,128)(2,1)} %bitcast.30), calls=%async_computation | async-start | bytes 2097152 | tf_op jit(solution)/shard_map/all_to_all | solution.py:442
  14.3 0.0 copy-done.3
  15.7 0.1 copy.16
  15.8 0.1 reshape.216
  15.9 0.1 add_select_fusion.2
  16.0 0.1 broadcast_multiply_fusion
  16.1 0.4 fusion.15
  16.5 0.0 copy-done.2
  16.5 1.4 %multiply_reduce_fusion = (f32[]{:T(128)}, f32[1,16384]{1,0:T(1,128)}) fusion(f32[1,16384]{1,0:T(1,128)S(1)} %copy-done.2, s32[]{:T(128)} %bitcast.31), kind=kLoop, calls=%fused_computation.20 | loop fusion | flops 65535 | bytes 131080 | tf_op jit(solution)/shard_map/reduce_sum | solution.py:449
  17.9 1.8 %fusion.7 = (f32[1,8,32,16]{3,2,1,0:T(8,128)S(1)}, f32[1,8,32,16]{3,2,1,0:T(8,128)S(1)}) fusion(s32[]{:T(128)S(6)} %select_n.109, s32[8,16]{1,0:T(8,128)S(1)} %add_select_fusion.2, s32[32]{0:T(128)S(1)} %get-tuple-element.5, f32[]{:T(128)S(6)} %div.13, pred[]{:T(512)S(6)} %lt.95), kind=kLoop, calls=%fused_computation.16 | loop fusion | flops 40960 | bytes 33417 | tf_op jit(solution)/shard_map/cos | solution.py:198
  19.7 0.6 pad_maximum_fusion.2.fine_ref
  27.2 0.7 pad_maximum_fusion.1.coarse_ref
  28.0 0.7 broadcast_in_dim.70.live_ref
  28.6 6.6 %shard_map.77 = bf16[32,128]{1,0:T(8,128)(2,1)} custom-call(bf16[64,16384]{1,0:T(8,128)(2,1)} %bitcast.42, f32[1,16384]{1,0:T(1,128)} %get-tuple-element.7.mask_ref, f32[2,32,128]{2,1,0:T(8,128)} %pad_maximum_fusion.2.fine_ref, f32[2,8,32,16]{3,2,1,0:T(8,128)} %pad_maximum_fusion.1.coarse_ref, f32[32,128]{1,0:T(8,128)} %broadcast_in_dim.70.live_ref), custom_call_target="tpu_custom_call" | custom-call | flops 134217728 | bytes 2097152 | tf_op jit(solution)/shard_map/pallas_call | solution.py:203
  35.3 0.5 compare_select_fusion.1
  35.8 3.1 %select_convert_fusion = bf16[16,128]{1,0:T(8,128)(2,1)S(1)} fusion(bf16[128]{0:T(256)(128)(2,1)S(1)} %compare_select_fusion.1, f32[]{:T(128)} %reduce_precision.22, bf16[]{:T(256)} %reduce_precision.23, f32[]{:T(128)} %reduce_precision.18, f32[]{:T(128)} %reduce_precision.19, bf16[]{:T(256)} %reduce_precision.20, pred[128]{0:T(512)(128)(4,1)S(1)} %get-tuple-element.12, ...), kind=kLoop, calls=%fused_computation.35 | loop fusion | flops 10240 | bytes 5008 | tf_op jit(solution)/shard_map/convert_element_type | solution.py:456
  38.9 0.7 pad_maximum_fusion.3
  39.6 22.2 %all_gather.3.gathered_ref = bf16[768,128]{1,0:T(8,128)(2,1)S(1)} all-gather(bf16[48,128]{1,0:T(8,128)(2,1)S(1)} %pad_maximum_fusion.3), channel_id=1, replica_groups=mesh['groups'=2,'band'=8,'sub'=2] {'band','sub'}, dimensions={0}, use_global_device_ids=true | all-gather | bytes 208896 | tf_op jit(solution)/shard_map/all_gather | solution.py:457
  61.9 0.0 copy-start.1
  61.9 0.1 copy.20
  62.0 0.7 slice_reduce_fusion
  64.0 0.7 pad_add_fusion.1.scalar_ref
  64.6 0.0 copy-done.1
  64.6 6.8 %shard_map.78 = f32[8192,128]{1,0:T(8,128)} custom-call(s32[2]{0:T(128)} %pad_add_fusion.1.scalar_ref, bf16[768,128]{1,0:T(8,128)(2,1)} %copy-done.1, bf16[32,8192]{1,0:T(8,128)(2,1)} %bitcast.37), custom_call_target="tpu_custom_call" | custom-call | flops 134217728 | bytes 4194304 | tf_op jit(solution)/shard_map/pallas_call | solution.py:271
  71.4 0.1 convert_reduce_fusion
  71.5 0.6 multiply_divide_fusion.scale_ref
  72.1 0.0 all-to-all-done
  72.1 0.0 copy-start
  72.1 1.0 copy-done
  73.1 31.2 %shard_map.79 = f32[8192,128]{1,0:T(8,128)} custom-call(f32[512]{0:T(512)} %multiply_divide_fusion.scale_ref, bf16[768,128]{1,0:T(8,128)(2,1)} %copy-done.1, bf16[1024,512]{1,0:T(8,128)(2,1)} %bitcast.38), custom_call_target="tpu_custom_call" | custom-call | flops 1073741824 | bytes 4194304 | tf_op jit(solution)/shard_map/pallas_call | solution.py:384
  (10 shorter events, 0.1 us)
Async XLA Ops:
  5.8 8.5 %copy-start.3 = (s32[16]{0:T(128)S(1)}, s32[16]{0:T(128)}, u32[]{:S(2)}) copy-start(s32[16]{0:T(128)} %param.10) | copy-start | bytes 196
  5.8 10.7 %copy-start.2 = (f32[1,16384]{1,0:T(1,128)S(1)}, f32[1,16384]{1,0:T(1,128)}, u32[]{:S(2)}) copy-start(f32[1,16384]{1,0:T(1,128)} %param.7) | copy-start | bytes 196612
  6.8 65.3 %all-to-all-start = ((bf16[16,64,512]{2,1,0:T(8,128)(2,1)}), bf16[16,64,512]{2,1,0:T(8,128)(2,1)S(1)}, u32[]{:S(2)}, u32[]{:S(2)}) async-start(bf16[16,64,512]{2,1,0:T(8,128)(2,1)} %bitcast.30), calls=%async_computation | async-start | bytes 2097152 | tf_op jit(solution)/shard_map/all_to_all | solution.py:442
  61.9 2.8 %copy-start.1 = (bf16[768,128]{1,0:T(8,128)(2,1)}, bf16[768,128]{1,0:T(8,128)(2,1)S(1)}, u32[]{:S(2)}) copy-start(bf16[768,128]{1,0:T(8,128)(2,1)S(1)} %all_gather.3.gathered_ref) | copy-start | bytes 589828
  72.1 1.0 copy-start

commit v2 on v1

--- a/solution.py
+++ b/solution.py
@@ -336,12 +336,12 @@
     per_batch = 128 // slots
     lane_group = lax.broadcasted_iota(jnp.int32, (8, 128), 1) // 32
 
-    def batch(position, carry):
+    def batch(position, buffer):
         rows = dense[pl.ds(pl.multiple_of(position * 128, 128), 128), :]
-        turned[...] = rows.T
+        turned[buffer * 128 : (buffer + 1) * 128, :] = rows.T
         left = jnp.concatenate(
             [
-                turned[pl.ds(32 * part + quarter, 8, stride=4), :]
+                turned[pl.ds(buffer * 128 + 32 * part + quarter, 8, stride=4), :]
                 for part in range(4)
                 for quarter in range(4)
             ],
@@ -370,9 +370,15 @@
                         value = pltpu.roll(value, 32 * turn, axis=1)
                     result = value if result is None else result + value
                 out_ref[pl.ds(degree * 16 + kind, 8, stride=2), :] = result * factor
+
+    together = 4
+
+    def several(position, carry):
+        for buffer in range(together):
+            batch(position * together + buffer, buffer)
         return carry
 
-    lax.fori_loop(0, height // per_batch, batch, 0, unroll=2)
+    lax.fori_loop(0, height // per_batch // together, several, 0)
 
 
 def spectra_call(scale, gathered, stride, legendre_rows):
@@ -395,7 +401,7 @@
             pltpu.VMEM(gathered.shape, jnp.float32),
             pltpu.VMEM((row_count, columns), jnp.bfloat16),
             pltpu.VMEM((height * slots, columns), jnp.float32),
-            pltpu.VMEM((128, 128), jnp.float32),
+            pltpu.VMEM((512, 128), jnp.float32),
         ],
         cost_estimate=pl.CostEstimate(
             flops=degree_local * slots * 4 * columns * columns,

time: 105 us -> 96.1 us (0.915)
  Pallas kernels: 44.6 us -> 35.5 us
    pallas_call x1, Pallas kernels: 31.2 us -> 22.1 us  [spectra_call(): pl.pallas_call(functools.partial(spectra_kernel, stride), grid=(degree_lo...]
  transfers between devices with their start and end apart: 1 -> 1, of which waited for: 0 -> 0; matrix products, arithmetic and copies ran while one was open for 12% -> 13% of each run, Pallas kernels for 13% -> 14%
where the time goes in v2:
time: 96.1 us; the launch traced here: 95.2 us
  Pallas kernels  35.5 us (37%)
  blocking collectives  22.2 us (23%)
  other arithmetic  14.1 us (15%)
  between operations  11.7 us (12%)
  starting transfers between devices  7.43 us (8%)
  local copies, waits for them, and re-layouts  4.24 us (4%)
    all_gather x1, blocking collectives, compact(): gathered = lax.all_gather(payload, axes, axis=0, tiled=True)  22.2 us
    pallas_call x1, Pallas kernels, spectra_call(): pl.pallas_call(functools.partial(spectra_kernel, stride), grid=(degree_lo...  22.1 us
    all_to_all x1, starting transfers between devices, compact(): lax.all_to_all(sent, axes, split_axis=0, concat_axis=0, tiled=True)  7.43 us
    pallas_call x1, Pallas kernels, alm_call(): pl.pallas_call(functools.partial(alm_kernel, stride), grid=(degree_count...  6.79 us
    pallas_call x1, Pallas kernels, fourier_call(): pl.pallas_call(fourier_kernel, grid=(blocks,), in_specs=[pl.BlockSpec((2...  6.62 us
    convert_element_type x1, other arithmetic, compact(): extra.astype(jnp.bfloat16)  3.09 us
  transfers between devices with their start and end apart: 1, of which 0 were waited for; matrix products, arithmetic and copies ran while one was open for 13% of the time, Pallas kernels for 14%

profile of v2, /device:TPU:0, one launch (start us, length us, event | category | flops | bytes accessed | tf_op | source)
XLA Modules:
  0.0 95.2 jit_solution(17056736891586816927)
XLA Ops:
  0.6 1.2 %dynamic_slice.7 = s32[1]{0:T(128)} dynamic-slice(s32[16]{0:T(128)} %param.10, s32[]{:T(128)S(6)} %select_n.107), dynamic_slice_sizes={1} | dynamic-slice | bytes 12 | tf_op jit(solution)/shard_map/jit(dynamic_index_in_dim)/dynamic_slice | solution.py:438
  1.9 0.7 iota_compare_fusion.1
  3.9 1.8 %fusion.1 = (bf16[32,8192]{1,0:T(8,128)(2,1)S(1)}, bf16[32,8192]{1,0:T(8,128)(2,1)S(1)}) fusion(s32[]{:T(128)S(6)} %select_n.121, bf16[32,8192]{1,0:T(8,128)(2,1)} %bitcast.36, pred[8192]{0:T(1024)(128)(4,1)S(1)} %iota_compare_fusion.1, bf16[1,8192,32]{1,2,0:T(8,128)(2,1)} %param.11, pred[8192]{0:T(1024)(128)(4,1)S(1)} %iota_compare_fusion), kind=kLoop, calls=%fused_computation.5 | loop fusion | flops 1572864 | bytes 2113540 | tf_op jit(solution)/shard_map/jit(_where)/select_n | solution.py:444
  5.7 0.1 pad_maximum_fusion
  5.8 0.0 copy-start.3
  5.8 0.0 copy-start.2
  5.8 1.1 %copy.23 = bf16[8,16,8,512]{3,2,0,1:T(8,128)(2,1)} copy(bf16[8,16,8,512]{3,2,1,0:T(8,128)(2,1)S(1)} %bitcast.41) | data formatting | bytes 2097152 | tf_op jit(solution)/shard_map/reshape | solution.py:447
  6.9 7.4 %all-to-all-start = ((bf16[16,64,512]{2,1,0:T(8,128)(2,1)}), bf16[16,64,512]{2,1,0:T(8,128)(2,1)S(1)}, u32[]{:S(2)}, u32[]{:S(2)}) async-start(bf16[16,64,512]{2,1,0:T(8,128)(2,1)} %bitcast.30), calls=%async_computation | async-start | bytes 2097152 | tf_op jit(solution)/shard_map/all_to_all | solution.py:448
  14.3 0.0 copy-done.3
  15.7 0.1 copy.16
  15.8 0.1 reshape.216
  15.9 0.1 add_select_fusion.2
  16.0 0.1 broadcast_multiply_fusion
  16.2 0.4 fusion.15
  16.5 0.0 copy-done.2
  16.5 1.4 %multiply_reduce_fusion = (f32[]{:T(128)}, f32[1,16384]{1,0:T(1,128)}) fusion(f32[1,16384]{1,0:T(1,128)S(1)} %copy-done.2, s32[]{:T(128)} %bitcast.31), kind=kLoop, calls=%fused_computation.20 | loop fusion | flops 65535 | bytes 131080 | tf_op jit(solution)/shard_map/reduce_sum | solution.py:455
  17.9 1.8 %fusion.7 = (f32[1,8,32,16]{3,2,1,0:T(8,128)S(1)}, f32[1,8,32,16]{3,2,1,0:T(8,128)S(1)}) fusion(s32[]{:T(128)S(6)} %select_n.109, s32[8,16]{1,0:T(8,128)S(1)} %add_select_fusion.2, s32[32]{0:T(128)S(1)} %get-tuple-element.5, f32[]{:T(128)S(6)} %div.13, pred[]{:T(512)S(6)} %lt.95), kind=kLoop, calls=%fused_computation.16 | loop fusion | flops 40960 | bytes 33417 | tf_op jit(solution)/shard_map/cos | solution.py:198
  19.7 0.6 pad_maximum_fusion.2.fine_ref
  27.3 0.7 pad_maximum_fusion.1.coarse_ref
  28.0 0.7 broadcast_in_dim.70.live_ref
  28.6 6.6 %shard_map.77 = bf16[32,128]{1,0:T(8,128)(2,1)} custom-call(bf16[64,16384]{1,0:T(8,128)(2,1)} %bitcast.42, f32[1,16384]{1,0:T(1,128)} %get-tuple-element.7.mask_ref, f32[2,32,128]{2,1,0:T(8,128)} %pad_maximum_fusion.2.fine_ref, f32[2,8,32,16]{3,2,1,0:T(8,128)} %pad_maximum_fusion.1.coarse_ref, f32[32,128]{1,0:T(8,128)} %broadcast_in_dim.70.live_ref), custom_call_target="tpu_custom_call" | custom-call | flops 134217728 | bytes 2097152 | tf_op jit(solution)/shard_map/pallas_call | solution.py:203
  35.3 0.5 compare_select_fusion.1
  35.9 3.1 %select_convert_fusion = bf16[16,128]{1,0:T(8,128)(2,1)S(1)} fusion(bf16[128]{0:T(256)(128)(2,1)S(1)} %compare_select_fusion.1, f32[]{:T(128)} %reduce_precision.22, bf16[]{:T(256)} %reduce_precision.23, f32[]{:T(128)} %reduce_precision.18, f32[]{:T(128)} %reduce_precision.19, bf16[]{:T(256)} %reduce_precision.20, pred[128]{0:T(512)(128)(4,1)S(1)} %get-tuple-element.12, ...), kind=kLoop, calls=%fused_computation.35 | loop fusion | flops 10240 | bytes 5008 | tf_op jit(solution)/shard_map/convert_element_type | solution.py:462
  38.9 0.7 pad_maximum_fusion.3
  39.6 22.2 %all_gather.3.gathered_ref = bf16[768,128]{1,0:T(8,128)(2,1)S(1)} all-gather(bf16[48,128]{1,0:T(8,128)(2,1)S(1)} %pad_maximum_fusion.3), channel_id=1, replica_groups=mesh['groups'=2,'band'=8,'sub'=2] {'band','sub'}, dimensions={0}, use_global_device_ids=true | all-gather | bytes 208896 | tf_op jit(solution)/shard_map/all_gather | solution.py:463
  61.9 0.0 copy-start.1
  61.9 0.1 copy.20
  62.0 0.7 slice_reduce_fusion
  64.0 0.7 pad_add_fusion.1.scalar_ref
  64.6 0.0 copy-done.1
  64.6 6.8 %shard_map.78 = f32[8192,128]{1,0:T(8,128)} custom-call(s32[2]{0:T(128)} %pad_add_fusion.1.scalar_ref, bf16[768,128]{1,0:T(8,128)(2,1)} %copy-done.1, bf16[32,8192]{1,0:T(8,128)(2,1)} %bitcast.37), custom_call_target="tpu_custom_call" | custom-call | flops 134217728 | bytes 4194304 | tf_op jit(solution)/shard_map/pallas_call | solution.py:271
  71.4 0.1 convert_reduce_fusion
  71.5 0.6 multiply_divide_fusion.scale_ref
  72.1 0.0 all-to-all-done
  72.1 0.0 copy-start
  72.1 1.0 %copy-done = bf16[16,64,512]{2,1,0:T(8,128)(2,1)} copy-done((bf16[16,64,512]{2,1,0:T(8,128)(2,1)}, bf16[16,64,512]{2,1,0:T(8,128)(2,1)S(1)}, u32[]{:S(2)}) %copy-start) | copy-done | bytes 1048600
  73.1 22.1 %shard_map.79 = f32[8192,128]{1,0:T(8,128)} custom-call(f32[512]{0:T(512)} %multiply_divide_fusion.scale_ref, bf16[768,128]{1,0:T(8,128)(2,1)} %copy-done.1, bf16[1024,512]{1,0:T(8,128)(2,1)} %bitcast.38), custom_call_target="tpu_custom_call" | custom-call | flops 1073741824 | bytes 4194304 | tf_op jit(solution)/shard_map/pallas_call | solution.py:390
  (10 shorter events, 0.1 us)
Async XLA Ops:
  5.8 8.5 %copy-start.3 = (s32[16]{0:T(128)S(1)}, s32[16]{0:T(128)}, u32[]{:S(2)}) copy-start(s32[16]{0:T(128)} %param.10) | copy-start | bytes 196
  5.8 10.7 %copy-start.2 = (f32[1,16384]{1,0:T(1,128)S(1)}, f32[1,16384]{1,0:T(1,128)}, u32[]{:S(2)}) copy-start(f32[1,16384]{1,0:T(1,128)} %param.7) | copy-start | bytes 196612
  6.9 65.3 %all-to-all-start = ((bf16[16,64,512]{2,1,0:T(8,128)(2,1)}), bf16[16,64,512]{2,1,0:T(8,128)(2,1)S(1)}, u32[]{:S(2)}, u32[]{:S(2)}) async-start(bf16[16,64,512]{2,1,0:T(8,128)(2,1)} %bitcast.30), calls=%async_computation | async-start | bytes 2097152 | tf_op jit(solution)/shard_map/all_to_all | solution.py:448
  61.9 2.8 %copy-start.1 = (bf16[768,128]{1,0:T(8,128)(2,1)}, bf16[768,128]{1,0:T(8,128)(2,1)S(1)}, u32[]{:S(2)}) copy-start(bf16[768,128]{1,0:T(8,128)(2,1)S(1)} %all_gather.3.gathered_ref) | copy-start | bytes 589828
  72.1 1.0 %copy-start = (bf16[16,64,512]{2,1,0:T(8,128)(2,1)}, bf16[16,64,512]{2,1,0:T(8,128)(2,1)S(1)}, u32[]{:S(2)}) copy-start(bf16[16,64,512]{2,1,0:T(8,128)(2,1)S(1)} %all-to-all-done) | copy-start | bytes 3145732

commit v3 on v2

--- a/solution.py
+++ b/solution.py
@@ -416,6 +416,60 @@
     )
 
 
+def gather_kernel(devices, subs, payload_ref, out_ref, send_sem, recv_sem):
+    me = lax.axis_index("band") * subs + lax.axis_index("sub")
+    rows = payload_ref.shape[0]
+
+    def place(index):
+        return {"band": index // subs, "sub": index % subs}
+
+    def slot(index):
+        return out_ref.at[pl.ds(pl.multiple_of(index * rows, rows), rows), :]
+
+    barrier = pltpu.get_barrier_semaphore()
+    for offset in range(1, devices):
+        pl.semaphore_signal(
+            barrier,
+            inc=1,
+            device_id=place((me + offset) % devices),
+            device_id_type=pl.DeviceIdType.MESH,
+        )
+    pl.semaphore_wait(barrier, devices - 1)
+
+    def copy_of(offset, source):
+        return pltpu.make_async_remote_copy(
+            src_ref=payload_ref,
+            dst_ref=slot(source),
+            send_sem=send_sem.at[offset],
+            recv_sem=recv_sem.at[offset],
+            device_id=place((me + offset) % devices),
+            device_id_type=pl.DeviceIdType.MESH,
+        )
+
+    for offset in range(1, devices):
+        copy_of(offset, me).start()
+    out_ref[pl.ds(pl.multiple_of(me * rows, rows), rows), :] = payload_ref[...]
+    for offset in range(1, devices):
+        copy_of(offset, (me + devices - offset) % devices).wait_recv()
+    for offset in range(1, devices):
+        copy_of(offset, me).wait_send()
+
+
+def gather_call(payload, devices, subs):
+    rows, columns = payload.shape
+    return pl.pallas_call(
+        functools.partial(gather_kernel, devices, subs),
+        in_specs=[pl.BlockSpec(memory_space=pltpu.VMEM)],
+        out_specs=pl.BlockSpec(memory_space=pltpu.VMEM),
+        out_shape=jax.ShapeDtypeStruct((devices * rows, columns), payload.dtype),
+        scratch_shapes=[
+            pltpu.SemaphoreType.DMA((devices,)),
+            pltpu.SemaphoreType.DMA((devices,)),
+        ],
+        compiler_params=pltpu.CompilerParams(collective_id=0, has_side_effects=True),
+    )(payload)
+
+
 def split_three(value):
     pieces = []
     rest = value
@@ -460,7 +514,7 @@
     for index, piece in enumerate(square + pixels):
         extra = jnp.where(column_index == index, piece, extra)
     payload = jnp.concatenate([coefficients, extra.astype(jnp.bfloat16)], axis=0)
-    gathered = lax.all_gather(payload, axes, axis=0, tiled=True)
+    gathered = gather_call(payload, devices, lax.axis_size("sub"))
     stride = slots + EXTRA
     pieces = gathered.reshape(devices, stride, columns)[:, slots, :6].astype(jnp.float32)
     weight = jnp.sum(pieces[:, :3]) / jnp.sum(pieces[:, 3:])

time: 96.1 us -> 85.6 us (0.89)
  blocking collectives: 22.2 us -> 0 us
  Pallas kernels: 35.5 us -> 45.5 us
    all_gather x1 -> x0, blocking collectives: 22.2 us -> none  [compact(): gathered = lax.all_gather(payload, axes, axis=0, tiled=True)]
    pallas_call x0 -> x1, Pallas kernels: none -> 10 us  [gather_call(): pl.pallas_call(functools.partial(gather_kernel, devices, subs), in_specs=...]
  transfers between devices with their start and end apart: 1 -> 1, of which waited for: 0 -> 0; matrix products, arithmetic and copies ran while one was open for 13% -> 16% of each run, Pallas kernels for 14% -> 28%
where the time goes in v3:
time: 85.6 us; the launch traced here: 84.6 us
  Pallas kernels  45.5 us (53%)
  other arithmetic  14.7 us (17%)
  between operations  12 us (14%)
  starting transfers between devices  7.44 us (9%)
  local copies, waits for them, and re-layouts  5.01 us (6%)
    pallas_call x1, Pallas kernels, spectra_call(): pl.pallas_call(functools.partial(spectra_kernel, stride), grid=(degree_lo...  22.1 us
    pallas_call x1, Pallas kernels, gather_call(): pl.pallas_call(functools.partial(gather_kernel, devices, subs), in_specs=...  10 us
    all_to_all x1, starting transfers between devices, compact(): lax.all_to_all(sent, axes, split_axis=0, concat_axis=0, tiled=True)  7.44 us
    pallas_call x1, Pallas kernels, alm_call(): pl.pallas_call(functools.partial(alm_kernel, stride), grid=(degree_count...  6.79 us
    pallas_call x1, Pallas kernels, fourier_call(): pl.pallas_call(fourier_kernel, grid=(blocks,), in_specs=[pl.BlockSpec((2...  6.62 us
    convert_element_type x1, other arithmetic, compact(): extra.astype(jnp.bfloat16)  3.07 us
    cos x1, other arithmetic, fourier_call(): coarse = jnp.stack([jnp.cos(coarse_angle), jnp.sin(coarse_angle)])  1.84 us
    select_n x1, other arithmetic, compact(): first = jnp.where(degrees >= first_order, rolled, 0.0).astype(jnp.bfloat16)  1.8 us
  transfers between devices with their start and end apart: 1, of which 0 were waited for; matrix products, arithmetic and copies ran while one was open for 16% of the time, Pallas kernels for 28%

profile of v3, /device:TPU:0, one launch (start us, length us, event | category | flops | bytes accessed | tf_op | source)
XLA Modules:
  0.0 84.6 jit_solution(16048966009969475636)
XLA Ops:
  0.6 1.2 %dynamic_slice.7 = s32[1]{0:T(128)} dynamic-slice(s32[16]{0:T(128)} %param.10, s32[]{:T(128)S(6)} %select_n.107), dynamic_slice_sizes={1} | dynamic-slice | bytes 12 | tf_op jit(solution)/shard_map/jit(dynamic_index_in_dim)/dynamic_slice | solution.py:492
  1.9 0.7 iota_compare_fusion.1
  3.9 1.8 %fusion.1 = (bf16[32,8192]{1,0:T(8,128)(2,1)S(1)}, bf16[32,8192]{1,0:T(8,128)(2,1)S(1)}) fusion(s32[]{:T(128)S(6)} %select_n.121, bf16[32,8192]{1,0:T(8,128)(2,1)} %bitcast.36, pred[8192]{0:T(1024)(128)(4,1)S(1)} %iota_compare_fusion.1, bf16[1,8192,32]{1,2,0:T(8,128)(2,1)} %param.11, pred[8192]{0:T(1024)(128)(4,1)S(1)} %iota_compare_fusion), kind=kLoop, calls=%fused_computation.5 | loop fusion | flops 1572864 | bytes 2113540 | tf_op jit(solution)/shard_map/jit(_where)/select_n | solution.py:498
  5.7 0.1 pad_maximum_fusion
  5.7 0.0 copy-start.2
  5.8 0.0 copy-start.1
  5.8 1.1 %copy.23 = bf16[8,16,8,512]{3,2,0,1:T(8,128)(2,1)} copy(bf16[8,16,8,512]{3,2,1,0:T(8,128)(2,1)S(1)} %bitcast.41) | data formatting | bytes 2097152 | tf_op jit(solution)/shard_map/reshape | solution.py:501
  6.8 7.4 %all-to-all-start = ((bf16[16,64,512]{2,1,0:T(8,128)(2,1)}), bf16[16,64,512]{2,1,0:T(8,128)(2,1)S(1)}, u32[]{:S(2)}, u32[]{:S(2)}) async-start(bf16[16,64,512]{2,1,0:T(8,128)(2,1)} %bitcast.30), calls=%async_computation | async-start | bytes 2097152 | tf_op jit(solution)/shard_map/all_to_all | solution.py:502
  14.3 0.0 copy-done.2
  15.6 0.1 copy.16
  15.7 0.1 reshape.216
  15.8 0.1 add_select_fusion.2
  15.9 0.1 broadcast_multiply_fusion
  16.1 0.3 fusion.15
  16.5 0.0 copy-done.1
  16.5 1.4 %multiply_reduce_fusion = (f32[]{:T(128)}, f32[1,16384]{1,0:T(1,128)}) fusion(f32[1,16384]{1,0:T(1,128)S(1)} %copy-done.1, s32[]{:T(128)} %bitcast.31), kind=kLoop, calls=%fused_computation.20 | loop fusion | flops 65535 | bytes 131080 | tf_op jit(solution)/shard_map/reduce_sum | solution.py:509
  17.8 1.8 %fusion.7 = (f32[1,8,32,16]{3,2,1,0:T(8,128)S(1)}, f32[1,8,32,16]{3,2,1,0:T(8,128)S(1)}) fusion(s32[]{:T(128)S(6)} %select_n.109, s32[8,16]{1,0:T(8,128)S(1)} %add_select_fusion.2, s32[32]{0:T(128)S(1)} %get-tuple-element.5, f32[]{:T(128)S(6)} %div.13, pred[]{:T(512)S(6)} %lt.95), kind=kLoop, calls=%fused_computation.16 | loop fusion | flops 40960 | bytes 33417 | tf_op jit(solution)/shard_map/cos | solution.py:198
  19.7 0.7 pad_maximum_fusion.1.coarse_ref
  20.4 0.6 pad_maximum_fusion.2.fine_ref
  28.2 0.7 broadcast_in_dim.70.live_ref
  28.9 6.6 %shard_map.77 = bf16[32,128]{1,0:T(8,128)(2,1)} custom-call(bf16[64,16384]{1,0:T(8,128)(2,1)} %bitcast.42, f32[1,16384]{1,0:T(1,128)} %get-tuple-element.7.mask_ref, f32[2,32,128]{2,1,0:T(8,128)} %pad_maximum_fusion.2.fine_ref, f32[2,8,32,16]{3,2,1,0:T(8,128)} %pad_maximum_fusion.1.coarse_ref, f32[32,128]{1,0:T(8,128)} %broadcast_in_dim.70.live_ref), custom_call_target="tpu_custom_call" | custom-call | flops 134217728 | bytes 2097152 | tf_op jit(solution)/shard_map/pallas_call | solution.py:203
  35.5 0.6 compare_select_fusion.1
  36.2 3.1 %select_convert_fusion = bf16[16,128]{1,0:T(8,128)(2,1)S(1)} fusion(bf16[128]{0:T(256)(128)(2,1)S(1)} %compare_select_fusion.1, f32[]{:T(128)} %reduce_precision.22, bf16[]{:T(256)} %reduce_precision.23, f32[]{:T(128)} %reduce_precision.18, f32[]{:T(128)} %reduce_precision.19, bf16[]{:T(256)} %reduce_precision.20, pred[128]{0:T(512)(128)(4,1)S(1)} %get-tuple-element.12, ...), kind=kLoop, calls=%fused_computation.35 | loop fusion | flops 10240 | bytes 5008 | tf_op jit(solution)/shard_map/convert_element_type | solution.py:516
  39.3 1.3 %pad_maximum_fusion.3.payload_ref = bf16[48,128]{1,0:T(8,128)(2,1)} fusion(bf16[16,128]{1,0:T(8,128)(2,1)S(1)} %select_convert_fusion, bf16[32,128]{1,0:T(8,128)(2,1)} %shard_map.77), kind=kLoop, calls=%fused_computation.34 | loop fusion | flops 24576 | bytes 24576 | tf_op jit(solution)/shard_map/concatenate | solution.py:516
  40.6 10.0 %shard_map.78.gathered_ref = bf16[768,128]{1,0:T(8,128)(2,1)} custom-call(bf16[48,128]{1,0:T(8,128)(2,1)} %pad_maximum_fusion.3.payload_ref), custom_call_target="tpu_custom_call" | custom-call | tf_op jit(solution)/shard_map/pallas_call | solution.py:460
  50.6 0.8 slice.12
  51.4 0.1 copy.20
  51.5 0.6 slice_reduce_fusion
  53.4 0.6 pad_add_fusion.1.scalar_ref
  54.0 6.8 %shard_map.79 = f32[8192,128]{1,0:T(8,128)} custom-call(s32[2]{0:T(128)} %pad_add_fusion.1.scalar_ref, bf16[768,128]{1,0:T(8,128)(2,1)} %shard_map.78.gathered_ref, bf16[32,8192]{1,0:T(8,128)(2,1)} %bitcast.37), custom_call_target="tpu_custom_call" | custom-call | flops 134217728 | bytes 4194304 | tf_op jit(solution)/shard_map/pallas_call | solution.py:271
  60.8 0.1 convert_reduce_fusion
  60.9 0.6 multiply_divide_fusion.scale_ref
  61.5 0.0 all-to-all-done
  61.5 0.0 copy-start
  61.5 1.0 %copy-done = bf16[16,64,512]{2,1,0:T(8,128)(2,1)} copy-done((bf16[16,64,512]{2,1,0:T(8,128)(2,1)}, bf16[16,64,512]{2,1,0:T(8,128)(2,1)S(1)}, u32[]{:S(2)}) %copy-start) | copy-done | bytes 1048600
  62.5 22.1 %shard_map.80 = f32[8192,128]{1,0:T(8,128)} custom-call(f32[512]{0:T(512)} %multiply_divide_fusion.scale_ref, bf16[768,128]{1,0:T(8,128)(2,1)} %shard_map.78.gathered_ref, bf16[1024,512]{1,0:T(8,128)(2,1)} %bitcast.38), custom_call_target="tpu_custom_call" | custom-call | flops 1073741824 | bytes 4194304 | tf_op jit(solution)/shard_map/pallas_call | solution.py:390
  (9 shorter events, 0.1 us)
Async XLA Ops:
  5.7 8.5 %copy-start.2 = (s32[16]{0:T(128)S(1)}, s32[16]{0:T(128)}, u32[]{:S(2)}) copy-start(s32[16]{0:T(128)} %param.10) | copy-start | bytes 196
  5.8 10.7 %copy-start.1 = (f32[1,16384]{1,0:T(1,128)S(1)}, f32[1,16384]{1,0:T(1,128)}, u32[]{:S(2)}) copy-start(f32[1,16384]{1,0:T(1,128)} %param.7) | copy-start | bytes 196612
  6.8 54.7 %all-to-all-start = ((bf16[16,64,512]{2,1,0:T(8,128)(2,1)}), bf16[16,64,512]{2,1,0:T(8,128)(2,1)S(1)}, u32[]{:S(2)}, u32[]{:S(2)}) async-start(bf16[16,64,512]{2,1,0:T(8,128)(2,1)} %bitcast.30), calls=%async_computation | async-start | bytes 2097152 | tf_op jit(solution)/shard_map/all_to_all | solution.py:502
  61.5 1.0 %copy-start = (bf16[16,64,512]{2,1,0:T(8,128)(2,1)}, bf16[16,64,512]{2,1,0:T(8,128)(2,1)S(1)}, u32[]{:S(2)}) copy-start(bf16[16,64,512]{2,1,0:T(8,128)(2,1)S(1)} %all-to-all-done) | copy-start | bytes 3145732

commit v4 on v3

--- a/solution.py
+++ b/solution.py
@@ -371,14 +371,14 @@
                     result = value if result is None else result + value
                 out_ref[pl.ds(degree * 16 + kind, 8, stride=2), :] = result * factor
 
-    together = 4
+    together = 8
 
     def several(position, carry):
         for buffer in range(together):
             batch(position * together + buffer, buffer)
         return carry
 
-    lax.fori_loop(0, height // per_batch // together, several, 0)
+    lax.fori_loop(0, height // (per_batch * together), several, 0)
 
 
 def spectra_call(scale, gathered, stride, legendre_rows):
@@ -401,7 +401,7 @@
             pltpu.VMEM(gathered.shape, jnp.float32),
             pltpu.VMEM((row_count, columns), jnp.bfloat16),
             pltpu.VMEM((height * slots, columns), jnp.float32),
-            pltpu.VMEM((512, 128), jnp.float32),
+            pltpu.VMEM((1024, 128), jnp.float32),
         ],
         cost_estimate=pl.CostEstimate(
             flops=degree_local * slots * 4 * columns * columns,

time: 85.6 us -> 81.1 us (0.947)
  Pallas kernels: 45.5 us -> 41 us
    pallas_call x1, Pallas kernels: 22.1 us -> 17.6 us  [spectra_call(): pl.pallas_call(functools.partial(spectra_kernel, stride), grid=(degree_lo...]
  transfers between devices with their start and end apart: 1 -> 1, of which waited for: 0 -> 0; matrix products, arithmetic and copies ran while one was open for 16% -> 17% of each run, Pallas kernels for 28% -> 29%
where the time goes in v4:
time: 81.1 us; the launch traced here: 80.1 us
  Pallas kernels  41 us (51%)
  other arithmetic  14.7 us (18%)
  between operations  12 us (15%)
  starting transfers between devices  7.41 us (9%)
  local copies, waits for them, and re-layouts  5.01 us (6%)
    pallas_call x1, Pallas kernels, spectra_call(): pl.pallas_call(functools.partial(spectra_kernel, stride), grid=(degree_lo...  17.6 us
    pallas_call x1, Pallas kernels, gather_call(): pl.pallas_call(functools.partial(gather_kernel, devices, subs), in_specs=...  10 us
    all_to_all x1, starting transfers between devices, compact(): lax.all_to_all(sent, axes, split_axis=0, concat_axis=0, tiled=True)  7.41 us
    pallas_call x1, Pallas kernels, alm_call(): pl.pallas_call(functools.partial(alm_kernel, stride), grid=(degree_count...  6.79 us
    pallas_call x1, Pallas kernels, fourier_call(): pl.pallas_call(fourier_kernel, grid=(blocks,), in_specs=[pl.BlockSpec((2...  6.62 us
    convert_element_type x1, other arithmetic, compact(): extra.astype(jnp.bfloat16)  3.07 us
    cos x1, other arithmetic, fourier_call(): coarse = jnp.stack([jnp.cos(coarse_angle), jnp.sin(coarse_angle)])  1.84 us
    select_n x1, other arithmetic, compact(): first = jnp.where(degrees >= first_order, rolled, 0.0).astype(jnp.bfloat16)  1.82 us
  transfers between devices with their start and end apart: 1, of which 0 were waited for; matrix products, arithmetic and copies ran while one was open for 17% of the time, Pallas kernels for 29%

profile of v4, /device:TPU:0, one launch (start us, length us, event | category | flops | bytes accessed | tf_op | source)
XLA Modules:
  0.0 80.1 jit_solution(4643685852238870045)
XLA Ops:
  0.6 1.2 %dynamic_slice.7 = s32[1]{0:T(128)} dynamic-slice(s32[16]{0:T(128)} %param.10, s32[]{:T(128)S(6)} %select_n.107), dynamic_slice_sizes={1} | dynamic-slice | bytes 12 | tf_op jit(solution)/shard_map/jit(dynamic_index_in_dim)/dynamic_slice | solution.py:492
  1.9 0.7 iota_compare_fusion.1
  3.9 1.8 %fusion.1 = (bf16[32,8192]{1,0:T(8,128)(2,1)S(1)}, bf16[32,8192]{1,0:T(8,128)(2,1)S(1)}) fusion(s32[]{:T(128)S(6)} %select_n.121, bf16[32,8192]{1,0:T(8,128)(2,1)} %bitcast.36, pred[8192]{0:T(1024)(128)(4,1)S(1)} %iota_compare_fusion.1, bf16[1,8192,32]{1,2,0:T(8,128)(2,1)} %param.11, pred[8192]{0:T(1024)(128)(4,1)S(1)} %iota_compare_fusion), kind=kLoop, calls=%fused_computation.5 | loop fusion | flops 1572864 | bytes 2113540 | tf_op jit(solution)/shard_map/jit(_where)/select_n | solution.py:498
  5.7 0.1 pad_maximum_fusion
  5.8 0.0 copy-start.2
  5.8 0.0 copy-start.1
  5.8 1.1 %copy.23 = bf16[8,16,8,512]{3,2,0,1:T(8,128)(2,1)} copy(bf16[8,16,8,512]{3,2,1,0:T(8,128)(2,1)S(1)} %bitcast.41) | data formatting | bytes 2097152 | tf_op jit(solution)/shard_map/reshape | solution.py:501
  6.9 7.4 %all-to-all-start = ((bf16[16,64,512]{2,1,0:T(8,128)(2,1)}), bf16[16,64,512]{2,1,0:T(8,128)(2,1)S(1)}, u32[]{:S(2)}, u32[]{:S(2)}) async-start(bf16[16,64,512]{2,1,0:T(8,128)(2,1)} %bitcast.30), calls=%async_computation | async-start | bytes 2097152 | tf_op jit(solution)/shard_map/all_to_all | solution.py:502
  14.3 0.0 copy-done.2
  15.6 0.1 copy.16
  15.7 0.1 reshape.216
  15.8 0.1 add_select_fusion.2
  15.9 0.1 broadcast_multiply_fusion
  16.1 0.3 fusion.15
  16.4 0.0 copy-done.1
  16.5 1.4 %multiply_reduce_fusion = (f32[]{:T(128)}, f32[1,16384]{1,0:T(1,128)}) fusion(f32[1,16384]{1,0:T(1,128)S(1)} %copy-done.1, s32[]{:T(128)} %bitcast.31), kind=kLoop, calls=%fused_computation.20 | loop fusion | flops 65535 | bytes 131080 | tf_op jit(solution)/shard_map/reduce_sum | solution.py:509
  17.8 1.8 %fusion.7 = (f32[1,8,32,16]{3,2,1,0:T(8,128)S(1)}, f32[1,8,32,16]{3,2,1,0:T(8,128)S(1)}) fusion(s32[]{:T(128)S(6)} %select_n.109, s32[8,16]{1,0:T(8,128)S(1)} %add_select_fusion.2, s32[32]{0:T(128)S(1)} %get-tuple-element.5, f32[]{:T(128)S(6)} %div.13, pred[]{:T(512)S(6)} %lt.95), kind=kLoop, calls=%fused_computation.16 | loop fusion | flops 40960 | bytes 33417 | tf_op jit(solution)/shard_map/cos | solution.py:198
  19.7 0.7 pad_maximum_fusion.1.coarse_ref
  20.4 0.6 pad_maximum_fusion.2.fine_ref
  28.2 0.7 broadcast_in_dim.70.live_ref
  28.9 6.6 %shard_map.77 = bf16[32,128]{1,0:T(8,128)(2,1)} custom-call(bf16[64,16384]{1,0:T(8,128)(2,1)} %bitcast.42, f32[1,16384]{1,0:T(1,128)} %get-tuple-element.7.mask_ref, f32[2,32,128]{2,1,0:T(8,128)} %pad_maximum_fusion.2.fine_ref, f32[2,8,32,16]{3,2,1,0:T(8,128)} %pad_maximum_fusion.1.coarse_ref, f32[32,128]{1,0:T(8,128)} %broadcast_in_dim.70.live_ref), custom_call_target="tpu_custom_call" | custom-call | flops 134217728 | bytes 2097152 | tf_op jit(solution)/shard_map/pallas_call | solution.py:203
  35.5 0.6 compare_select_fusion.1
  36.2 3.1 %select_convert_fusion = bf16[16,128]{1,0:T(8,128)(2,1)S(1)} fusion(bf16[128]{0:T(256)(128)(2,1)S(1)} %compare_select_fusion.1, f32[]{:T(128)} %reduce_precision.22, bf16[]{:T(256)} %reduce_precision.23, f32[]{:T(128)} %reduce_precision.18, f32[]{:T(128)} %reduce_precision.19, bf16[]{:T(256)} %reduce_precision.20, pred[128]{0:T(512)(128)(4,1)S(1)} %get-tuple-element.12, ...), kind=kLoop, calls=%fused_computation.35 | loop fusion | flops 10240 | bytes 5008 | tf_op jit(solution)/shard_map/convert_element_type | solution.py:516
  39.3 1.3 %pad_maximum_fusion.3.payload_ref = bf16[48,128]{1,0:T(8,128)(2,1)} fusion(bf16[16,128]{1,0:T(8,128)(2,1)S(1)} %select_convert_fusion, bf16[32,128]{1,0:T(8,128)(2,1)} %shard_map.77), kind=kLoop, calls=%fused_computation.34 | loop fusion | flops 24576 | bytes 24576 | tf_op jit(solution)/shard_map/concatenate | solution.py:516
  40.6 10.0 %shard_map.78.gathered_ref = bf16[768,128]{1,0:T(8,128)(2,1)} custom-call(bf16[48,128]{1,0:T(8,128)(2,1)} %pad_maximum_fusion.3.payload_ref), custom_call_target="tpu_custom_call" | custom-call | tf_op jit(solution)/shard_map/pallas_call | solution.py:460
  50.6 0.8 slice.12
  51.3 0.1 copy.20
  51.5 0.6 slice_reduce_fusion
  53.4 0.6 pad_add_fusion.1.scalar_ref
  54.0 6.8 %shard_map.79 = f32[8192,128]{1,0:T(8,128)} custom-call(s32[2]{0:T(128)} %pad_add_fusion.1.scalar_ref, bf16[768,128]{1,0:T(8,128)(2,1)} %shard_map.78.gathered_ref, bf16[32,8192]{1,0:T(8,128)(2,1)} %bitcast.37), custom_call_target="tpu_custom_call" | custom-call | flops 134217728 | bytes 4194304 | tf_op jit(solution)/shard_map/pallas_call | solution.py:271
  60.8 0.1 convert_reduce_fusion
  60.9 0.6 multiply_divide_fusion.scale_ref
  61.5 0.0 all-to-all-done
  61.5 0.0 copy-start
  61.5 1.0 %copy-done = bf16[16,64,512]{2,1,0:T(8,128)(2,1)} copy-done((bf16[16,64,512]{2,1,0:T(8,128)(2,1)}, bf16[16,64,512]{2,1,0:T(8,128)(2,1)S(1)}, u32[]{:S(2)}) %copy-start) | copy-done | bytes 1048600
  62.5 17.6 %shard_map.80 = f32[8192,128]{1,0:T(8,128)} custom-call(f32[512]{0:T(512)} %multiply_divide_fusion.scale_ref, bf16[768,128]{1,0:T(8,128)(2,1)} %shard_map.78.gathered_ref, bf16[1024,512]{1,0:T(8,128)(2,1)} %bitcast.38), custom_call_target="tpu_custom_call" | custom-call | flops 1073741824 | bytes 4194304 | tf_op jit(solution)/shard_map/pallas_call | solution.py:390
  (9 shorter events, 0.1 us)
Async XLA Ops:
  5.8 8.5 %copy-start.2 = (s32[16]{0:T(128)S(1)}, s32[16]{0:T(128)}, u32[]{:S(2)}) copy-start(s32[16]{0:T(128)} %param.10) | copy-start | bytes 196
  5.8 10.7 %copy-start.1 = (f32[1,16384]{1,0:T(1,128)S(1)}, f32[1,16384]{1,0:T(1,128)}, u32[]{:S(2)}) copy-start(f32[1,16384]{1,0:T(1,128)} %param.7) | copy-start | bytes 196612
  6.9 54.7 %all-to-all-start = ((bf16[16,64,512]{2,1,0:T(8,128)(2,1)}), bf16[16,64,512]{2,1,0:T(8,128)(2,1)S(1)}, u32[]{:S(2)}, u32[]{:S(2)}) async-start(bf16[16,64,512]{2,1,0:T(8,128)(2,1)} %bitcast.30), calls=%async_computation | async-start | bytes 2097152 | tf_op jit(solution)/shard_map/all_to_all | solution.py:502
  61.5 1.0 %copy-start = (bf16[16,64,512]{2,1,0:T(8,128)(2,1)}, bf16[16,64,512]{2,1,0:T(8,128)(2,1)S(1)}, u32[]{:S(2)}) copy-start(bf16[16,64,512]{2,1,0:T(8,128)(2,1)S(1)} %all-to-all-done) | copy-start | bytes 3145732
